TPU v7x, 32 devices: a whole 2x2x4 slice. The times are simulated.
32 devices in a mesh: sec: 4 (over y, core), grp: 8 (over z, x).
Axes of the slice: x: 2, y: 2, z: 4, core: 2. Of those that a mesh axis runs over, the one named last changes fastest.
Arguments:
- solution_in: float32 [2, 32, 4, 6144], P(None, 'grp', None, 'sec'), may hold values from -6 to 6
- residual_in: float32 [2, 32, 4, 6144], P(None, 'grp', None, 'sec'), may hold values from -6 to 6
- direction_in: float32 [2, 32, 4, 6144], P(None, 'grp', None, 'sec'), may hold values from -6 to 6
- legendre: bfloat16 [32, 2, 128, 6144], P('grp', None, None, 'sec'), may hold values from -0.0034179688 to 0.0034179688
- inverse_prior: float32 [2, 6144], P(None, 'sec'), may hold values from 0.3 to 10
- noise_qq: float32 [128, 8192], P('grp', 'sec'), may hold values from 0.5 to 4
- noise_qu: float32 [128, 8192], P('grp', 'sec'), may hold values from -0.3 to 0.3
- noise_uu: float32 [128, 8192], P('grp', 'sec'), may hold values from 0.5 to 4
- pixel_mask: int32 [128, 8192], P('grp', 'sec'), may hold values 0 or 1
- cycle_phase: float32 [128], replicated, as said below
- m_values: int32 [32], replicated, may hold values from 0 to 6143, as said below
Outputs:
- solution: float32 [2, 32, 4, 6144], P(None, 'grp', None, 'sec')
- residual: float32 [2, 32, 4, 6144], P(None, 'grp', None, 'sec')
- direction: float32 [2, 32, 4, 6144], P(None, 'grp', None, 'sec')
Inputs may be any that keep to these rules, and one draw needn't show every extreme that they name: `m_values`: the slots' m values are distinct, and exactly one slot has m = 0. `cycle_phase`: each phase lies between 0 and 2 pi / 8192.
All inputs are finite; a program needn't handle non-finite values. No bound on the sum of `pixel_mask` on one device may be relied on, other than what follows from the above.
Results may differ from a plain program's by a relative error of at most 0.025.
Values sent between devices are 32-bit elements; how exact they have to be, the bound alone decides.
No kernel may reach another device: no remote copies, remote signals or barrier semaphores. Data moves between devices by JAX's collectives and lax.ppermute only.
A program may use at most 64 MiB of HBM per device.

v0:
```python
import math
import jax
import jax.numpy as jnp
from jax import lax
from jax.sharding import PartitionSpec as P

ITERS = 4
full_turn = 2.0 * math.pi


def combine_modes(prod):
    plus = prod[:, :, 0]
    minus = prod[:, :, 1]
    return jnp.stack(
        [
            -plus[:, :, 0] + minus[:, :, 3],
            -plus[:, :, 1] - minus[:, :, 2],
            -plus[:, :, 2] - minus[:, :, 1],
            -plus[:, :, 3] + minus[:, :, 0],
        ],
        axis=2,
    )


def adjoint_terms(field):
    half = field.astype(jnp.bfloat16)
    minus_part = jnp.stack([half[:, :, 3], -half[:, :, 2], -half[:, :, 1], half[:, :, 0]], axis=2)
    return jnp.stack([-half, minus_part], axis=2)


def legendre_forward(coeffs, legendre):
    half = coeffs.astype(jnp.bfloat16)
    prod = jnp.einsum("msrl,bmcl->bmscr", legendre, half, preferred_element_type=jnp.float32)
    return combine_modes(prod)


def legendre_adjoint(field, legendre):
    both = adjoint_terms(field)
    return jnp.einsum("msrl,bmscr->bmcl", legendre, both, preferred_element_type=jnp.float32)


def phi_table(m_values, start, count, total):
    index = start + jnp.arange(count, dtype=jnp.int32)
    folded = m_values[:, None] * index[None, :] % total
    angle = folded.astype(jnp.float32) * (full_turn / total)
    weight = jnp.where(m_values == 0, 1.0, 2.0).astype(jnp.float32)[:, None]
    return jnp.concatenate([weight * jnp.cos(angle), -weight * jnp.sin(angle)], axis=0)


def pixel_segment(field, cosines, sine_table, table, noise_qq, noise_qu, noise_uu, mask_f):
    count = field.shape[0]
    modes = field.shape[1]
    cycles = field.shape[3]
    parts = field.reshape(count, modes, 2, 2, cycles)
    real = parts[:, :, :, 0]
    imag = parts[:, :, :, 1]
    cosm = cosines[None, :, None, :]
    sinm = sine_table[None, :, None, :]
    rot_re = real * cosm - imag * sinm
    rot_im = real * sinm + imag * cosm
    rows = (
        jnp.stack([rot_re, rot_im], axis=1)
        .transpose(0, 3, 4, 1, 2)
        .reshape(count * 2 * cycles, 2 * modes)
    )
    pixels = jnp.dot(
        rows, table, precision=lax.Precision.HIGHEST, preferred_element_type=jnp.float32
    )
    pixels = pixels.reshape(count, 2, cycles, -1)
    qpart = pixels[:, 0]
    upart = pixels[:, 1]
    wq = mask_f * (noise_qq * qpart + noise_qu * upart)
    wu = mask_f * (noise_qu * qpart + noise_uu * upart)
    weighted = jnp.stack([wq, wu], axis=1).reshape(count * 2 * cycles, -1)
    back = jnp.dot(
        weighted, table.T, precision=lax.Precision.HIGHEST, preferred_element_type=jnp.float32
    )
    back = back.reshape(count, 2, cycles, 2, modes)
    out = jnp.stack([back[:, :, :, 0], back[:, :, :, 1]], axis=2)
    return out.transpose(0, 4, 1, 2, 3).reshape(count, modes, 4, cycles)


def rotate_back(field, cosines, sine_table):
    count = field.shape[0]
    modes = field.shape[1]
    cycles = field.shape[3]
    parts = field.reshape(count, modes, 2, 2, cycles)
    real = parts[:, :, :, 0]
    imag = parts[:, :, :, 1]
    cosm = cosines[None, :, None, :]
    sinm = sine_table[None, :, None, :]
    turned_real = real * cosm + imag * sinm
    turned_imag = imag * cosm - real * sinm
    return jnp.stack([turned_real, turned_imag], axis=3).reshape(count, modes, 4, cycles)


def totals(values):
    return jnp.sum(values, axis=(1, 2, 3))


def per_device(
    solution_in,
    residual_in,
    direction_in,
    legendre,
    inverse_prior,
    noise_qq,
    noise_qu,
    noise_uu,
    pixel_mask,
    cycle_phase,
    m_values,
):
    phi_local = noise_qq.shape[1]
    cycles_here = noise_qq.shape[0]
    modes_here = solution_in.shape[1]
    sections = lax.axis_size("sec")
    group_index = lax.axis_index("grp")
    local_phase = lax.dynamic_slice_in_dim(cycle_phase, group_index * cycles_here, cycles_here, 0)
    angle = m_values.astype(jnp.float32)[:, None] * local_phase[None, :]
    cosines = jnp.cos(angle)
    sine_table = jnp.sin(angle)
    local_m = lax.dynamic_slice_in_dim(m_values, group_index * modes_here, modes_here, 0)
    slot_angle = local_m.astype(jnp.float32)[:, None] * cycle_phase[None, :]
    slot_cos = jnp.cos(slot_angle)
    slot_sin = jnp.sin(slot_angle)
    mask_f = pixel_mask.astype(jnp.float32)
    prior = jnp.repeat(inverse_prior, 2, axis=0)[None, None]
    table = phi_table(m_values, lax.axis_index("sec") * phi_local, phi_local, phi_local * sections)
    solution, residual, direction = (solution_in, residual_in, direction_in)
    for step in range(ITERS):
        apply_field = legendre_forward(direction, legendre)
        field = lax.all_to_all(apply_field, "grp", split_axis=3, concat_axis=1, tiled=True)
        field = lax.psum(field, "sec")
        partial_field = pixel_segment(
            field, cosines, sine_table, table, noise_qq, noise_qu, noise_uu, mask_f
        )
        folded = lax.all_to_all(partial_field, "grp", split_axis=1, concat_axis=3, tiled=True)
        folded = lax.psum(folded, "sec")
        mode_field = rotate_back(folded, slot_cos, slot_sin)
        image = prior * direction + legendre_adjoint(mode_field, legendre)
        norm_now, curve, cross, square = lax.psum(
            (
                totals(residual * residual),
                totals(direction * image),
                totals(residual * image),
                totals(image * image),
            ),
            ("sec", "grp"),
        )
        step_size = norm_now / curve
        alpha = step_size[:, None, None, None]
        solution = solution + alpha * direction
        residual = residual - alpha * image
        norm_next = norm_now - 2.0 * step_size * cross + step_size * step_size * square
        direction = residual + (norm_next / norm_now)[:, None, None, None] * direction
    return (solution, residual, direction)


def solution(mesh):
    return jax.shard_map(
        per_device,
        mesh=mesh,
        in_specs=(
            P(None, "grp", None, "sec"),
            P(None, "grp", None, "sec"),
            P(None, "grp", None, "sec"),
            P("grp", None, None, "sec"),
            P(None, "sec"),
            P("grp", "sec"),
            P("grp", "sec"),
            P("grp", "sec"),
            P("grp", "sec"),
            P(),
            P(),
        ),
        out_specs=(
            P(None, "grp", None, "sec"),
            P(None, "grp", None, "sec"),
            P(None, "grp", None, "sec"),
        ),
        check_vma=False,
    )
```

profile of v0, /device:TPU:0, one launch (start us, length us, event | category | flops | bytes accessed | tf_op | source)
XLA Modules:
  0.0 451.1 jit_solution(6203677750327580794)
XLA Ops:
  5.5 2.4 reshape.484
  7.9 7.3 %all-to-all-start = ((f32[8,1,512]{2,1,0:T(1,128)}), f32[8,1,512]{2,1,0:T(1,128)S(1)}, u32[]{:S(2)}, u32[]{:S(2)}) async-start(f32[8,1,512]{2,1,0:T(1,128)} %reshape.484), calls=%async_computation | async-start | bytes 32768 | tf_op jit(solution)/shard_map/all_to_all | solution.py:133
  24.6 2.2 copy.135
  26.8 12.4 %psum.169 = f32[2,32,2,2,16]{4,1,3,2,0:T(8,128)} all-reduce(f32[2,32,2,2,16]{4,1,3,2,0:T(8,128)} %bitcast.348), channel_id=1, replica_groups=mesh['sec'=4,'grp'=8] {'sec'}, use_global_device_ids=true, to_apply=%region_2.3 | all-reduce | flops 4096 | bytes 32768 | tf_op jit(solution)/shard_map/psum | solution.py:134
  45.3 2.5 fusion.52
  50.2 4.5 all-to-all-start.1
  55.8 5.5 %all-to-all-done.1 = f32[8,1,512]{2,1,0:T(1,128)S(1)} async-done(((f32[8,1,512]{2,1,0:T(1,128)}), f32[8,1,512]{2,1,0:T(1,128)S(1)}, u32[]{:S(2)}, u32[]{:S(2)}) %all-to-all-start.1) | async-done | bytes 16416 | tf_op jit(solution)/shard_map/all_to_all | solution.py:138
  65.4 10.1 %psum.170 = f32[2,4,2,2,128]{4,3,2,1,0:T(2,128)S(1)} all-reduce(f32[2,4,2,2,128]{4,3,2,1,0:T(2,128)S(1)} %reshape.451), channel_id=1, replica_groups=mesh['sec'=4,'grp'=8] {'sec'}, use_global_device_ids=true, to_apply=%region_3.4 | all-reduce | flops 4096 | bytes 32768 | tf_op jit(solution)/shard_map/psum | solution.py:139
  75.6 2.2 multiply_reduce_fusion.12
  77.9 38.3 %all-reduce.3 = (f32[2]{0:T(128)S(1)}, f32[2]{0:T(128)S(1)}, f32[2]{0:T(128)S(1)}, f32[2]{0:T(128)S(1)}) all-reduce(f32[2]{0:T(128)S(1)} %multiply_reduce_fusion.15, f32[2]{0:T(128)S(1)} %get-tuple-element.29, f32[2]{0:T(128)S(1)} %get-tuple-element.28, f32[2]{0:T(128)S(1)} %get-tuple-element.27), channel_id=1, replica_groups=mesh['sec'=4,'grp'=8] {'sec','grp'}, use_global_device_ids=true, to_apply=%region_1.2 | all-reduce | flops 8 | bytes 64 | tf_op jit(solution)/shard_map/psum | solution.py:142
  122.7 10.9 %all_to_all.144 = f32[8,1,512]{2,1,0:T(1,128)S(1)} all-to-all(f32[8,1,512]{2,1,0:T(1,128)S(1)} %reshape.488), channel_id=1, replica_groups=mesh['sec'=4,'grp'=8] {'grp'}, dimensions={0} | all-to-all | bytes 32768 | tf_op jit(solution)/shard_map/all_to_all | solution.py:133
  135.9 2.2 copy.153
  139.7 12.6 %psum.175 = f32[2,32,2,2,16]{4,1,2,0,3:T(8,128)} all-reduce(f32[2,32,2,2,16]{4,1,2,0,3:T(8,128)} %copy.154), channel_id=1, replica_groups=mesh['sec'=4,'grp'=8] {'sec'}, use_global_device_ids=true, to_apply=%region_12.13 | all-reduce | flops 4096 | bytes 32768 | tf_op jit(solution)/shard_map/psum | solution.py:134
  158.4 2.5 fusion.55
  162.7 8.9 %all_to_all.145 = f32[8,1,512]{2,1,0:T(1,128)S(1)} all-to-all(f32[8,1,512]{2,1,0:T(1,128)S(1)} %reshape.490), channel_id=1, replica_groups=mesh['sec'=4,'grp'=8] {'grp'}, dimensions={0} | all-to-all | bytes 32768 | tf_op jit(solution)/shard_map/all_to_all | solution.py:138
  175.7 10.1 %psum.176 = f32[2,4,2,2,128]{4,3,2,1,0:T(2,128)S(1)} all-reduce(f32[2,4,2,2,128]{4,3,2,1,0:T(2,128)S(1)} %reshape.454), channel_id=1, replica_groups=mesh['sec'=4,'grp'=8] {'sec'}, use_global_device_ids=true, to_apply=%region_13.14 | all-reduce | flops 4096 | bytes 32768 | tf_op jit(solution)/shard_map/psum | solution.py:139
  186.0 2.2 multiply_reduce_fusion.8
  188.2 38.7 %all-reduce.2 = (f32[2]{0:T(128)S(1)}, f32[2]{0:T(128)S(1)}, f32[2]{0:T(128)S(1)}, f32[2]{0:T(128)S(1)}) all-reduce(f32[2]{0:T(128)S(1)} %get-tuple-element.26, f32[2]{0:T(128)S(1)} %get-tuple-element.25, f32[2]{0:T(128)S(1)} %get-tuple-element.24, f32[2]{0:T(128)S(1)} %get-tuple-element.23), channel_id=1, replica_groups=mesh['sec'=4,'grp'=8] {'sec','grp'}, use_global_device_ids=true, to_apply=%region_7.8 | all-reduce | flops 8 | bytes 64 | tf_op jit(solution)/shard_map/psum | solution.py:142
  233.4 10.9 %all_to_all.146 = f32[8,1,512]{2,1,0:T(1,128)S(1)} all-to-all(f32[8,1,512]{2,1,0:T(1,128)S(1)} %reshape.492), channel_id=1, replica_groups=mesh['sec'=4,'grp'=8] {'grp'}, dimensions={0} | all-to-all | bytes 32768 | tf_op jit(solution)/shard_map/all_to_all | solution.py:133
  250.4 12.4 %psum.181 = f32[2,32,2,2,16]{4,1,2,0,3:T(8,128)} all-reduce(f32[2,32,2,2,16]{4,1,2,0,3:T(8,128)} %copy.166), channel_id=1, replica_groups=mesh['sec'=4,'grp'=8] {'sec'}, use_global_device_ids=true, to_apply=%region_22.23 | all-reduce | flops 4096 | bytes 32768 | tf_op jit(solution)/shard_map/psum | solution.py:134
  268.9 2.5 fusion.58
  273.2 8.9 %all_to_all.147 = f32[8,1,512]{2,1,0:T(1,128)S(1)} all-to-all(f32[8,1,512]{2,1,0:T(1,128)S(1)} %reshape.494), channel_id=1, replica_groups=mesh['sec'=4,'grp'=8] {'grp'}, dimensions={0} | all-to-all | bytes 32768 | tf_op jit(solution)/shard_map/all_to_all | solution.py:138
  286.2 10.1 %psum.182 = f32[2,4,2,2,128]{4,3,2,1,0:T(2,128)S(1)} all-reduce(f32[2,4,2,2,128]{4,3,2,1,0:T(2,128)S(1)} %reshape.457), channel_id=1, replica_groups=mesh['sec'=4,'grp'=8] {'sec'}, use_global_device_ids=true, to_apply=%region_23.24 | all-reduce | flops 4096 | bytes 32768 | tf_op jit(solution)/shard_map/psum | solution.py:139
  296.5 2.2 multiply_reduce_fusion.4
  298.7 38.7 %all-reduce.1 = (f32[2]{0:T(128)S(1)}, f32[2]{0:T(128)S(1)}, f32[2]{0:T(128)S(1)}, f32[2]{0:T(128)S(1)}) all-reduce(f32[2]{0:T(128)S(1)} %get-tuple-element.22, f32[2]{0:T(128)S(1)} %get-tuple-element.21, f32[2]{0:T(128)S(1)} %get-tuple-element.20, f32[2]{0:T(128)S(1)} %get-tuple-element.19), channel_id=1, replica_groups=mesh['sec'=4,'grp'=8] {'sec','grp'}, use_global_device_ids=true, to_apply=%region_17.18 | all-reduce | flops 8 | bytes 64 | tf_op jit(solution)/shard_map/psum | solution.py:142
  344.0 10.9 %all_to_all.148 = f32[8,1,512]{2,1,0:T(1,128)S(1)} all-to-all(f32[8,1,512]{2,1,0:T(1,128)S(1)} %reshape.496), channel_id=1, replica_groups=mesh['sec'=4,'grp'=8] {'grp'}, dimensions={0} | all-to-all | bytes 32768 | tf_op jit(solution)/shard_map/all_to_all | solution.py:133
  361.0 12.4 %psum.187 = f32[2,32,2,2,16]{4,1,2,0,3:T(8,128)} all-reduce(f32[2,32,2,2,16]{4,1,2,0,3:T(8,128)} %copy.178), channel_id=1, replica_groups=mesh['sec'=4,'grp'=8] {'sec'}, use_global_device_ids=true, to_apply=%region_32.33 | all-reduce | flops 4096 | bytes 32768 | tf_op jit(solution)/shard_map/psum | solution.py:134
  378.8 2.5 fusion.61
  383.1 8.9 %all_to_all.149 = f32[8,1,512]{2,1,0:T(1,128)S(1)} all-to-all(f32[8,1,512]{2,1,0:T(1,128)S(1)} %reshape.498), channel_id=1, replica_groups=mesh['sec'=4,'grp'=8] {'grp'}, dimensions={0} | all-to-all | bytes 32768 | tf_op jit(solution)/shard_map/all_to_all | solution.py:138
  396.1 10.1 %psum.188 = f32[2,4,2,2,128]{4,3,2,1,0:T(2,128)S(1)} all-reduce(f32[2,4,2,2,128]{4,3,2,1,0:T(2,128)S(1)} %reshape.460), channel_id=1, replica_groups=mesh['sec'=4,'grp'=8] {'sec'}, use_global_device_ids=true, to_apply=%region_33.34 | all-reduce | flops 4096 | bytes 32768 | tf_op jit(solution)/shard_map/psum | solution.py:139
  406.4 2.2 multiply_reduce_fusion.1
  408.7 38.7 %all-reduce = (f32[2]{0:T(128)S(1)}, f32[2]{0:T(128)S(1)}, f32[2]{0:T(128)S(1)}, f32[2]{0:T(128)S(1)}) all-reduce(f32[2]{0:T(128)S(1)} %get-tuple-element.18, f32[2]{0:T(128)S(1)} %get-tuple-element.17, f32[2]{0:T(128)S(1)} %get-tuple-element.16, f32[2]{0:T(128)S(1)} %get-tuple-element.15), channel_id=1, replica_groups=mesh['sec'=4,'grp'=8] {'sec','grp'}, use_global_device_ids=true, to_apply=%region_27.28 | all-reduce | flops 8 | bytes 64 | tf_op jit(solution)/shard_map/psum | solution.py:142
  (168 shorter events, 102.4 us)
Async XLA Ops:
  0.6 1.9 copy-start
  0.6 14.5 %copy-start.7 = (s32[32]{0:T(128)S(1)}, s32[32]{0:T(128)}, u32[]{:S(2)}) copy-start(s32[32]{0:T(128)} %param.21) | copy-start | bytes 388
  0.7 14.6 %copy-start.8 = (f32[128]{0:T(128)S(1)}, f32[128]{0:T(128)}, u32[]{:S(2)}) copy-start(f32[128]{0:T(128)} %param.20) | copy-start | bytes 1540
  7.9 13.9 %all-to-all-start = ((f32[8,1,512]{2,1,0:T(1,128)}), f32[8,1,512]{2,1,0:T(1,128)S(1)}, u32[]{:S(2)}, u32[]{:S(2)}) async-start(f32[8,1,512]{2,1,0:T(1,128)} %reshape.484), calls=%async_computation | async-start | bytes 32768 | tf_op jit(solution)/shard_map/all_to_all | solution.py:133
  16.6 0.7 copy-start.1
  24.6 31.2 %copy-start.6 = (f32[2,1536]{1,0:T(2,128)S(1)}, f32[2,1536]{1,0:T(2,128)}, u32[]{:S(2)}) copy-start(f32[2,1536]{1,0:T(2,128)} %param.15) | copy-start | bytes 36868
  50.2 11.1 %all-to-all-start.1 = ((f32[8,1,512]{2,1,0:T(1,128)}), f32[8,1,512]{2,1,0:T(1,128)S(1)}, u32[]{:S(2)}, u32[]{:S(2)}) async-start(f32[8,1,512]{2,1,0:T(1,128)} %reshape.486), calls=%async_computation.1 | async-start | bytes 32768 | tf_op jit(solution)/shard_map/all_to_all | solution.py:138
  118.2 0.7 copy-start.2
  228.9 0.7 copy-start.4
  339.4 0.7 copy-start.5
  378.8 68.6 %copy-start.3 = (f32[2,4,4,1536]{3,2,0,1:T(4,128)S(1)}, f32[2,4,4,1536]{3,2,0,1:T(4,128)}, u32[]{:S(2)}) copy-start(f32[2,4,4,1536]{3,2,0,1:T(4,128)} %copy-done.2) | copy-start | bytes 589828
where the time goes:
time: 454 us; the launch traced here: 451 us
  blocking collectives  304 us (67%)
  local copies, waits for them, and re-layouts  67 us (15%)
  matrix products  29.7 us (7%)
  other arithmetic  29.5 us (6%)
  starting transfers between devices  11.8 us (3%)
  waiting for transfers between devices  7.35 us (2%)
    psum x4, blocking collectives, per_device(): lax.psum((totals(residual * residual), totals(direction * image), totals(...  155 us
    psum x4, blocking collectives, per_device(): field = lax.psum(field, 'sec')  49.9 us
    psum x4, blocking collectives, per_device(): folded = lax.psum(folded, 'sec')  40.5 us
    all_to_all x3, blocking collectives, per_device(): lax.all_to_all(apply_field, 'grp', split_axis=3, concat_axis=1, tiled=True)  32.7 us
    unnamed x37, local copies, waits for them, and re-layouts  28.9 us
    all_to_all x3, blocking collectives, per_device(): lax.all_to_all(partial_field, 'grp', split_axis=1, concat_axis=3, tiled=T...  26.8 us
    dot_general x4, matrix products, pixel_segment(): jnp.dot(weighted, table.T, precision=lax.Precision.HIGHEST, preferred_ele...  9.92 us
    all_to_all x5, local copies, waits for them, and re-layouts, per_device(): lax.all_to_all(apply_field, 'grp', split_axis=3, concat_axis=1, tiled=True)  9.38 us
  transfers between devices with their start and end apart: 2, of which 2 were waited for; matrix products, arithmetic and copies ran while one was open for 1% of the time, Pallas kernels for 0%

commit v1 on v0

--- a/solution.py
+++ b/solution.py
@@ -1,11 +1,26 @@
+import functools
 import math
 import jax
 import jax.numpy as jnp
 from jax import lax
 from jax.sharding import PartitionSpec as P
+from jax.lax import axis_size, ppermute
 
 ITERS = 4
 full_turn = 2.0 * math.pi
+
+
+def perform_digits(row_data, axis_key):
+    how_many = axis_size(axis_key)
+    seen_now, s_next = (row_data, 0)
+    while 1 << s_next < how_many:
+        k_now = ppermute(seen_now, axis_key, [(s, s ^ 1 << s_next) for s in range(how_many)])
+        seen_now = seen_now + k_now
+        s_next = s_next + 1
+    return seen_now
+
+
+take_threads = functools.partial(perform_digits, axis_key="sec")
 
 
 def combine_modes(prod):
@@ -136,7 +151,7 @@
             field, cosines, sine_table, table, noise_qq, noise_qu, noise_uu, mask_f
         )
         folded = lax.all_to_all(partial_field, "grp", split_axis=1, concat_axis=3, tiled=True)
-        folded = lax.psum(folded, "sec")
+        folded = take_threads(folded)
         mode_field = rotate_back(folded, slot_cos, slot_sin)
         image = prior * direction + legendre_adjoint(mode_field, legendre)
         norm_now, curve, cross, square = lax.psum(

time: 454 us -> 433 us (0.954)
  blocking collectives: 304 us -> 264 us
  waiting for transfers between devices: 7.35 us -> 19.4 us
  starting transfers between devices: 11.8 us -> 19.5 us
    psum x4 -> x0, blocking collectives: 40.5 us -> none  [per_device(): folded = lax.psum(folded, 'sec')]
    ppermute x0 -> x8, waiting for transfers between devices: none -> 10.8 us  [perform_digits(): ppermute(seen_now, axis_key, [(s, s ^ 1 << s_next) for s in range(how_man...]
    ppermute x0 -> x8, starting transfers between devices: none -> 7.86 us  [perform_digits(): ppermute(seen_now, axis_key, [(s, s ^ 1 << s_next) for s in range(how_man...]
    all_to_all x8 -> x12, local copies, waits for them, and re-layouts: 6.35 us -> 10.4 us  [per_device(): lax.all_to_all(partial_field, 'grp', split_axis=1, concat_axis=3, tiled=T...]
  transfers between devices with their start and end apart: 2 -> 10, of which waited for: 2 -> 10; matrix products, arithmetic and copies ran while one was open for 1% -> 1% of each run, Pallas kernels for 0% -> 0%
where the time goes in v1:
time: 433 us; the launch traced here: 430 us
  blocking collectives  264 us (61%)
  local copies, waits for them, and re-layouts  66.9 us (15%)
  matrix products  29.6 us (7%)
  other arithmetic  29.5 us (7%)
  starting transfers between devices  19.5 us (5%)
  waiting for transfers between devices  19.4 us (4%)
    psum x4, blocking collectives, per_device(): lax.psum((totals(residual * residual), totals(direction * image), totals(...  155 us
    psum x4, blocking collectives, per_device(): field = lax.psum(field, 'sec')  49.9 us
    all_to_all x3, blocking collectives, per_device(): lax.all_to_all(apply_field, 'grp', split_axis=3, concat_axis=1, tiled=True)  32.7 us
    unnamed x37, local copies, waits for them, and re-layouts  28.9 us
    all_to_all x3, blocking collectives, per_device(): lax.all_to_all(partial_field, 'grp', split_axis=1, concat_axis=3, tiled=T...  26.8 us
    ppermute x8, waiting for transfers between devices, perform_digits(): ppermute(seen_now, axis_key, [(s, s ^ 1 << s_next) for s in range(how_man...  10.8 us
    all_to_all x12, local copies, waits for them, and re-layouts, per_device(): lax.all_to_all(partial_field, 'grp', split_axis=1, concat_axis=3, tiled=T...  10.4 us
    dot_general x4, matrix products, pixel_segment(): jnp.dot(weighted, table.T, precision=lax.Precision.HIGHEST, preferred_ele...  9.88 us
  transfers between devices with their start and end apart: 10, of which 10 were waited for; matrix products, arithmetic and copies ran while one was open for 1% of the time, Pallas kernels for 0%

profile of v1, /device:TPU:0, one launch (start us, length us, event | category | flops | bytes accessed | tf_op | source)
XLA Modules:
  0.0 430.4 jit_solution(11527141634017926927)
XLA Ops:
  5.5 2.4 reshape.480
  7.9 7.3 %all-to-all-start = ((f32[8,1,512]{2,1,0:T(1,128)}), f32[8,1,512]{2,1,0:T(1,128)S(1)}, u32[]{:S(2)}, u32[]{:S(2)}) async-start(f32[8,1,512]{2,1,0:T(1,128)} %reshape.480), calls=%async_computation | async-start | bytes 32768 | tf_op jit(solution)/shard_map/all_to_all | solution.py:148
  19.7 2.1 all-to-all-done
  24.6 2.2 copy.135
  26.8 12.4 %psum.141 = f32[2,32,2,2,16]{4,1,3,2,0:T(8,128)} all-reduce(f32[2,32,2,2,16]{4,1,3,2,0:T(8,128)} %bitcast.352), channel_id=1, replica_groups=mesh['sec'=4,'grp'=8] {'sec'}, use_global_device_ids=true, to_apply=%region_2.3 | all-reduce | flops 4096 | bytes 32768 | tf_op jit(solution)/shard_map/psum | solution.py:149
  45.3 2.5 fusion.52
  50.2 4.3 %all-to-all-start.1 = ((f32[8,1,512]{2,1,0:T(1,128)}), f32[8,1,512]{2,1,0:T(1,128)S(1)}, u32[]{:S(2)}, u32[]{:S(2)}) async-start(f32[8,1,512]{2,1,0:T(1,128)} %reshape.482), calls=%async_computation.1 | async-start | bytes 32768 | tf_op jit(solution)/shard_map/all_to_all | solution.py:153
  54.6 6.5 %all-to-all-done.1 = f32[8,1,512]{2,1,0:T(1,128)S(1)} async-done(((f32[8,1,512]{2,1,0:T(1,128)}), f32[8,1,512]{2,1,0:T(1,128)S(1)}, u32[]{:S(2)}, u32[]{:S(2)}) %all-to-all-start.1) | async-done | bytes 16416 | tf_op jit(solution)/shard_map/all_to_all | solution.py:153
  70.3 2.2 multiply_reduce_fusion.12
  72.6 38.3 %all-reduce.3 = (f32[2]{0:T(128)S(1)}, f32[2]{0:T(128)S(1)}, f32[2]{0:T(128)S(1)}, f32[2]{0:T(128)S(1)}) all-reduce(f32[2]{0:T(128)S(1)} %multiply_reduce_fusion.15, f32[2]{0:T(128)S(1)} %get-tuple-element.29, f32[2]{0:T(128)S(1)} %get-tuple-element.28, f32[2]{0:T(128)S(1)} %get-tuple-element.27), channel_id=1, replica_groups=mesh['sec'=4,'grp'=8] {'sec','grp'}, use_global_device_ids=true, to_apply=%region_1.2 | all-reduce | flops 8 | bytes 64 | tf_op jit(solution)/shard_map/psum | solution.py:157
  117.4 10.9 %all_to_all.144 = f32[8,1,512]{2,1,0:T(1,128)S(1)} all-to-all(f32[8,1,512]{2,1,0:T(1,128)S(1)} %reshape.484), channel_id=1, replica_groups=mesh['sec'=4,'grp'=8] {'grp'}, dimensions={0} | all-to-all | bytes 32768 | tf_op jit(solution)/shard_map/all_to_all | solution.py:148
  130.6 2.2 copy.153
  134.4 12.6 %psum.146 = f32[2,32,2,2,16]{4,1,2,0,3:T(8,128)} all-reduce(f32[2,32,2,2,16]{4,1,2,0,3:T(8,128)} %copy.154), channel_id=1, replica_groups=mesh['sec'=4,'grp'=8] {'sec'}, use_global_device_ids=true, to_apply=%region_11.12 | all-reduce | flops 4096 | bytes 32768 | tf_op jit(solution)/shard_map/psum | solution.py:149
  153.1 2.5 fusion.55
  157.4 8.9 %all_to_all.145 = f32[8,1,512]{2,1,0:T(1,128)S(1)} all-to-all(f32[8,1,512]{2,1,0:T(1,128)S(1)} %reshape.486), channel_id=1, replica_groups=mesh['sec'=4,'grp'=8] {'grp'}, dimensions={0} | all-to-all | bytes 32768 | tf_op jit(solution)/shard_map/all_to_all | solution.py:153
  175.6 2.2 multiply_reduce_fusion.8
  177.8 38.7 %all-reduce.2 = (f32[2]{0:T(128)S(1)}, f32[2]{0:T(128)S(1)}, f32[2]{0:T(128)S(1)}, f32[2]{0:T(128)S(1)}) all-reduce(f32[2]{0:T(128)S(1)} %get-tuple-element.26, f32[2]{0:T(128)S(1)} %get-tuple-element.25, f32[2]{0:T(128)S(1)} %get-tuple-element.24, f32[2]{0:T(128)S(1)} %get-tuple-element.23), channel_id=1, replica_groups=mesh['sec'=4,'grp'=8] {'sec','grp'}, use_global_device_ids=true, to_apply=%region_6.7 | all-reduce | flops 8 | bytes 64 | tf_op jit(solution)/shard_map/psum | solution.py:157
  223.0 10.9 %all_to_all.146 = f32[8,1,512]{2,1,0:T(1,128)S(1)} all-to-all(f32[8,1,512]{2,1,0:T(1,128)S(1)} %reshape.488), channel_id=1, replica_groups=mesh['sec'=4,'grp'=8] {'grp'}, dimensions={0} | all-to-all | bytes 32768 | tf_op jit(solution)/shard_map/all_to_all | solution.py:148
  236.3 2.2 copy.165
  240.0 12.4 %psum.151 = f32[2,32,2,2,16]{4,1,2,0,3:T(8,128)} all-reduce(f32[2,32,2,2,16]{4,1,2,0,3:T(8,128)} %copy.166), channel_id=1, replica_groups=mesh['sec'=4,'grp'=8] {'sec'}, use_global_device_ids=true, to_apply=%region_20.21 | all-reduce | flops 4096 | bytes 32768 | tf_op jit(solution)/shard_map/psum | solution.py:149
  258.5 2.5 fusion.58
  262.8 8.9 %all_to_all.147 = f32[8,1,512]{2,1,0:T(1,128)S(1)} all-to-all(f32[8,1,512]{2,1,0:T(1,128)S(1)} %reshape.490), channel_id=1, replica_groups=mesh['sec'=4,'grp'=8] {'grp'}, dimensions={0} | all-to-all | bytes 32768 | tf_op jit(solution)/shard_map/all_to_all | solution.py:153
  277.1 2.0 collective-permute-start.5
  281.0 2.2 multiply_reduce_fusion.4
  283.2 38.8 %all-reduce.1 = (f32[2]{0:T(128)S(1)}, f32[2]{0:T(128)S(1)}, f32[2]{0:T(128)S(1)}, f32[2]{0:T(128)S(1)}) all-reduce(f32[2]{0:T(128)S(1)} %get-tuple-element.22, f32[2]{0:T(128)S(1)} %get-tuple-element.21, f32[2]{0:T(128)S(1)} %get-tuple-element.20, f32[2]{0:T(128)S(1)} %get-tuple-element.19), channel_id=1, replica_groups=mesh['sec'=4,'grp'=8] {'sec','grp'}, use_global_device_ids=true, to_apply=%region_15.16 | all-reduce | flops 8 | bytes 64 | tf_op jit(solution)/shard_map/psum | solution.py:157
  328.4 10.9 %all_to_all.148 = f32[8,1,512]{2,1,0:T(1,128)S(1)} all-to-all(f32[8,1,512]{2,1,0:T(1,128)S(1)} %reshape.492), channel_id=1, replica_groups=mesh['sec'=4,'grp'=8] {'grp'}, dimensions={0} | all-to-all | bytes 32768 | tf_op jit(solution)/shard_map/all_to_all | solution.py:148
  341.7 2.2 copy.177
  345.4 12.4 %psum.156 = f32[2,32,2,2,16]{4,1,2,0,3:T(8,128)} all-reduce(f32[2,32,2,2,16]{4,1,2,0,3:T(8,128)} %copy.178), channel_id=1, replica_groups=mesh['sec'=4,'grp'=8] {'sec'}, use_global_device_ids=true, to_apply=%region_29.30 | all-reduce | flops 4096 | bytes 32768 | tf_op jit(solution)/shard_map/psum | solution.py:149
  363.3 2.5 fusion.61
  367.6 8.9 %all_to_all.149 = f32[8,1,512]{2,1,0:T(1,128)S(1)} all-to-all(f32[8,1,512]{2,1,0:T(1,128)S(1)} %reshape.494), channel_id=1, replica_groups=mesh['sec'=4,'grp'=8] {'grp'}, dimensions={0} | all-to-all | bytes 32768 | tf_op jit(solution)/shard_map/all_to_all | solution.py:153
  385.7 2.2 multiply_reduce_fusion.1
  388.0 38.8 %all-reduce = (f32[2]{0:T(128)S(1)}, f32[2]{0:T(128)S(1)}, f32[2]{0:T(128)S(1)}, f32[2]{0:T(128)S(1)}) all-reduce(f32[2]{0:T(128)S(1)} %get-tuple-element.18, f32[2]{0:T(128)S(1)} %get-tuple-element.17, f32[2]{0:T(128)S(1)} %get-tuple-element.16, f32[2]{0:T(128)S(1)} %get-tuple-element.15), channel_id=1, replica_groups=mesh['sec'=4,'grp'=8] {'sec','grp'}, use_global_device_ids=true, to_apply=%region_24.25 | all-reduce | flops 8 | bytes 64 | tf_op jit(solution)/shard_map/psum | solution.py:157
  (184 shorter events, 112.8 us)
Async XLA Ops:
  0.6 1.9 copy-start
  0.6 14.5 %copy-start.7 = (s32[32]{0:T(128)S(1)}, s32[32]{0:T(128)}, u32[]{:S(2)}) copy-start(s32[32]{0:T(128)} %param.21) | copy-start | bytes 388
  0.7 14.5 %copy-start.8 = (f32[128]{0:T(128)S(1)}, f32[128]{0:T(128)}, u32[]{:S(2)}) copy-start(f32[128]{0:T(128)} %param.20) | copy-start | bytes 1540
  7.9 13.9 %all-to-all-start = ((f32[8,1,512]{2,1,0:T(1,128)}), f32[8,1,512]{2,1,0:T(1,128)S(1)}, u32[]{:S(2)}, u32[]{:S(2)}) async-start(f32[8,1,512]{2,1,0:T(1,128)} %reshape.480), calls=%async_computation | async-start | bytes 32768 | tf_op jit(solution)/shard_map/all_to_all | solution.py:148
  16.4 0.7 copy-start.1
  40.1 29.0 %copy-start.6 = (f32[2,1536]{1,0:T(2,128)S(1)}, f32[2,1536]{1,0:T(2,128)}, u32[]{:S(2)}) copy-start(f32[2,1536]{1,0:T(2,128)} %param.15) | copy-start | bytes 36868
  50.2 10.9 %all-to-all-start.1 = ((f32[8,1,512]{2,1,0:T(1,128)}), f32[8,1,512]{2,1,0:T(1,128)S(1)}, u32[]{:S(2)}, u32[]{:S(2)}) async-start(f32[8,1,512]{2,1,0:T(1,128)} %reshape.482), calls=%async_computation.1 | async-start | bytes 32768 | tf_op jit(solution)/shard_map/all_to_all | solution.py:153
  65.2 1.2 collective-permute-start
  66.4 3.7 collective-permute-start.1
  112.9 0.7 copy-start.2
  170.4 1.2 collective-permute-start.2
  171.7 3.7 collective-permute-start.3
  218.5 0.7 copy-start.4
  275.8 1.2 collective-permute-start.4
  277.1 3.7 collective-permute-start.5
  323.9 0.7 copy-start.5
  365.7 61.0 %copy-start.3 = (f32[2,4,4,1536]{3,2,0,1:T(4,128)S(1)}, f32[2,4,4,1536]{3,2,0,1:T(4,128)}, u32[]{:S(2)}) copy-start(f32[2,4,4,1536]{3,2,0,1:T(4,128)} %copy-done.2) | copy-start | bytes 589828
  380.6 1.2 collective-permute-start.6
  381.8 3.7 collective-permute-start.7
